TPU v7x, 512 devices: a whole 4x8x8 slice. The times are simulated.
512 devices in a mesh: tick: 64 (over y, z_hi, core), wire: 8 (over z_lo, x).
Axes of the slice: x: 4, y: 8, z: 8 (z_hi: 4, z_lo: 2; z = z_hi * 2 + z_lo), core: 2. Of those that a mesh axis runs over, the one named last changes fastest.
Arguments:
- signal: float32 [16, 512, 8192], P(None, 'wire', 'tick'), may hold values from -6 to 6
- kernel_front: float32 [16, 3, 9], replicated, may hold values from -1.25 to 1.25
- mixing_front: float32 [16, 16], replicated, may hold values from -1.5 to 1.5
- offset_front: float32 [16], replicated, may hold values from -2 to 2
- kernel_back: float32 [16, 3, 9], replicated, may hold values from -1.25 to 1.25
- mixing_back: float32 [16, 16], replicated, may hold values from -1.5 to 1.5
- offset_back: float32 [16], replicated, may hold values from -2 to 2
- upstream: float32 [16, 512, 8192], P(None, 'wire', 'tick'), may hold values from -13 to 13
Outputs:
- response: float32 [16, 512, 8192], P(None, 'wire', 'tick')
- signal_grad: float32 [16, 512, 8192], P(None, 'wire', 'tick')
- kernel_front_grad: float32 [16, 3, 9], replicated
- mixing_front_grad: float32 [16, 16], replicated
- offset_front_grad: float32 [16], replicated
- kernel_back_grad: float32 [16, 3, 9], replicated
- mixing_back_grad: float32 [16, 16], replicated
- offset_back_grad: float32 [16], replicated
All inputs are finite; a program needn't handle non-finite values.
Results may differ from a plain program's by a relative error of at most 0.0003.
Values sent between devices are 32-bit elements; how exact they have to be, the bound alone decides.
No kernel may reach another device: no remote copies, remote signals or barrier semaphores. Data moves between devices by JAX's collectives and lax.ppermute only.
A program may use at most 64 MiB of HBM per device.

v0:
```python
import math
import jax
import jax.numpy as jnp
from jax import lax
from jax.sharding import PartitionSpec as P

TICK_DILATION = 8


def with_halo(block, sides, width):
    for axis, dim in sides:
        count = lax.axis_size(axis)
        forward = [(i, i + 1) for i in range(count - 1)]
        backward = [(target, source) for source, target in forward]
        low = lax.ppermute(
            lax.slice_in_dim(block, block.shape[dim] - width, None, axis=dim), axis, forward
        )
        high = lax.ppermute(lax.slice_in_dim(block, 0, width, axis=dim), axis, backward)
        block = jnp.concatenate([low, block, high], axis=dim)
    return block


def spread(field, tick_deep, wire_deep):
    longer = with_halo(field, (("tick", 2),), tick_deep)
    return with_halo(longer, (("wire", 1),), wire_deep)


def depthwise(padded_input, kernel_weight, row_count, column_count):
    total_sum = jnp.zeros((padded_input.shape[0], row_count, column_count), jnp.float32)
    for row_index in range(3):
        for column_index in range(9):
            total_sum = (
                total_sum
                + kernel_weight[:, row_index, column_index][:, None, None]
                * padded_input[
                    :,
                    row_index : row_index + row_count,
                    TICK_DILATION * column_index : TICK_DILATION * column_index + column_count,
                ]
            )
    return total_sum


def tap_grads(upward_gradient, padded_input):
    row_count = upward_gradient.shape[1]
    column_count = upward_gradient.shape[2]
    text_lines = []
    for row_index in range(3):
        text_lines.append(
            jnp.stack(
                [
                    jnp.sum(
                        upward_gradient
                        * padded_input[
                            :,
                            row_index : row_index + row_count,
                            TICK_DILATION * column_index : TICK_DILATION * column_index
                            + column_count,
                        ],
                        axis=(1, 2),
                    )
                    for column_index in range(9)
                ],
                axis=1,
            )
        )
    return jnp.stack(text_lines, axis=1)


def mixing(matrix, field, offset):
    return (
        jnp.einsum("oc,cwt->owt", matrix, field, precision=lax.Precision.HIGHEST)
        + offset[:, None, None]
    )


def slope(preact):
    sig = jax.nn.sigmoid(preact)
    return sig * (1.0 + preact * (1.0 - sig))


def per_device(
    signal,
    kernel_front,
    mixing_front,
    offset_front,
    kernel_back,
    mixing_back,
    offset_back,
    upstream,
):
    row_count = signal.shape[1]
    column_count = signal.shape[2]
    kernel_extent = 4 * TICK_DILATION
    padded_in = spread(signal, kernel_extent, 1)
    taps_front = depthwise(padded_in, kernel_front, row_count, column_count)
    pre_front = mixing(mixing_front, taps_front, offset_front)
    padded_act = spread(jax.nn.silu(pre_front), kernel_extent, 1)
    taps_back = depthwise(padded_act, kernel_back, row_count, column_count)
    pre_back = mixing(mixing_back, taps_back, offset_back)
    response = jax.nn.silu(pre_back)
    grad_back = upstream * slope(pre_back)
    gmix_back = jnp.einsum("owt,cwt->oc", grad_back, taps_back, precision=lax.Precision.HIGHEST)
    gbias_back = jnp.sum(grad_back, axis=(1, 2))
    under_back = jnp.einsum("oc,owt->cwt", mixing_back, grad_back, precision=lax.Precision.HIGHEST)
    gkern_back = tap_grads(under_back, padded_act)
    into_front = depthwise(
        spread(under_back, kernel_extent, 1), kernel_back[:, ::-1, ::-1], row_count, column_count
    )
    grad_front = into_front * slope(pre_front)
    gmix_front = jnp.einsum("owt,cwt->oc", grad_front, taps_front, precision=lax.Precision.HIGHEST)
    gbias_front = jnp.sum(grad_front, axis=(1, 2))
    under_front = jnp.einsum(
        "oc,owt->cwt", mixing_front, grad_front, precision=lax.Precision.HIGHEST
    )
    gkern_front = tap_grads(under_front, padded_in)
    signal_grad = depthwise(
        spread(under_front, kernel_extent, 1), kernel_front[:, ::-1, ::-1], row_count, column_count
    )
    totals = lax.psum(
        (gkern_front, gmix_front, gbias_front, gkern_back, gmix_back, gbias_back), ("tick", "wire")
    )
    factor = 1.0 / math.sqrt(
        row_count * lax.axis_size("wire") * column_count * lax.axis_size("tick")
    )
    return (
        response,
        signal_grad,
        totals[0] * factor,
        totals[1] * factor,
        totals[2] * factor,
        totals[3] * factor,
        totals[4] * factor,
        totals[5] * factor,
    )


def solution(mesh):
    in_specs = (P(None, "wire", "tick"), P(), P(), P(), P(), P(), P(), P(None, "wire", "tick"))
    out_specs = (P(None, "wire", "tick"), P(None, "wire", "tick"), P(), P(), P(), P(), P(), P())
    return jax.shard_map(
        per_device, mesh=mesh, in_specs=in_specs, out_specs=out_specs, check_vma=False
    )
```

profile of v0, /device:TPU:30, one launch (start us, length us, event | category | flops | bytes accessed | tf_op | source)
XLA Modules:
  0.0 259.0 jit_solution(9432671093252713411)
XLA Ops:
  4.1 10.3 %collective-permute-start.1 = (f32[16,64,32]{2,0,1:T(8,128)S(1)}, f32[16,64,32]{2,0,1:T(8,128)S(1)}, u32[]{:S(2)}, u32[]{:S(2)}) collective-permute-start(f32[16,64,32]{2,0,1:T(8,128)S(1)} %get-tuple-element.132), channel_id=1, source_target_pairs={{8,0},{16,8},{24,16},{32,24},{40,32},{48,40},{56,48},{64,56},{72,6... | collective-permute-start | bytes 393224 | tf_op jit(solution)/shard_map/ppermute | solution.py:18
  14.5 9.6 %collective-permute-done = f32[16,64,32]{2,0,1:T(8,128)S(1)} collective-permute-done((f32[16,64,32]{2,0,1:T(8,128)S(1)}, f32[16,64,32]{2,0,1:T(8,128)S(1)}, u32[]{:S(2)}, u32[]{:S(2)}) %collective-permute-start) | collective-permute-done | bytes 131104 | tf_op jit(solution)/shard_map/ppermute | solution.py:15
  25.4 2.9 %collective-permute-start.2 = (f32[16,1,192]{2,0,1:T(8,128)S(1)}, f32[16,1,192]{2,0,1:T(8,128)S(1)}, u32[]{:S(2)}, u32[]{:S(2)}) collective-permute-start(f32[16,1,192]{2,0,1:T(8,128)S(1)} %get-tuple-element.120), channel_id=1, source_target_pairs={{0,1},{1,2},{2,3},{3,4},{4,5},{5,6},{6,7},{8,9},{9,10},{10,11},{11... | collective-permute-start | bytes 36872 | tf_op jit(solution)/shard_map/ppermute | solution.py:15
  28.3 2.9 %collective-permute-start.3 = (f32[16,1,192]{2,0,1:T(8,128)S(1)}, f32[16,1,192]{2,0,1:T(8,128)S(1)}, u32[]{:S(2)}, u32[]{:S(2)}) collective-permute-start(f32[16,1,192]{2,0,1:T(8,128)S(1)} %get-tuple-element.121), channel_id=1, source_target_pairs={{1,0},{2,1},{3,2},{4,3},{5,4},{6,5},{7,6},{9,8},{10,9},{11,10},{12... | collective-permute-start | bytes 36872 | tf_op jit(solution)/shard_map/ppermute | solution.py:18
  31.3 4.7 %collective-permute-done.3 = f32[16,1,192]{2,0,1:T(8,128)S(1)} collective-permute-done((f32[16,1,192]{2,0,1:T(8,128)S(1)}, f32[16,1,192]{2,0,1:T(8,128)S(1)}, u32[]{:S(2)}, u32[]{:S(2)}) %collective-permute-start.3) | collective-permute-done | bytes 12320 | tf_op jit(solution)/shard_map/ppermute | solution.py:18
  37.0 3.9 %multiply_add_fusion.1 = f32[16,64,128]{2,0,1:T(8,128)S(1)} fusion(f32[16,64,128]{2,0,1:T(8,128)S(1)} %get-tuple-element.130, f32[16,65,192]{2,0,1:T(8,128)S(1)} %get-tuple-element.119, f32[16,64,160]{2,0,1:T(8,128)S(1)} %constant_dynamic-update-slice_fusion, f32[16,65,192]{2,0,1:T(8,128)S(1)} %get-tuple-element.118, f32[16]{0:T(128)S(1)} %get-tuple-element.185, ...), kind=kLoop, calls=%fused_computation.251 | loop fusion | flops 7471104 | bytes 12715712 | tf_op jit(solution)/shard_map/add | solution.py:33
  42.6 2.4 collective-permute-start.4
  45.1 6.1 %collective-permute-start.5 = (f32[16,64,32]{2,0,1:T(8,128)S(1)}, f32[16,64,32]{2,0,1:T(8,128)S(1)}, u32[]{:S(2)}, u32[]{:S(2)}) collective-permute-start(f32[16,64,32]{2,0,1:T(8,128)S(1)} %get-tuple-element.128), channel_id=1, source_target_pairs={{8,0},{16,8},{24,16},{32,24},{40,32},{48,40},{56,48},{64,56},{72,6... | collective-permute-start | bytes 393224 | tf_op jit(solution)/shard_map/ppermute | solution.py:18
  51.2 7.9 %collective-permute-done.4 = f32[16,64,32]{2,0,1:T(8,128)S(1)} collective-permute-done((f32[16,64,32]{2,0,1:T(8,128)S(1)}, f32[16,64,32]{2,0,1:T(8,128)S(1)}, u32[]{:S(2)}, u32[]{:S(2)}) %collective-permute-start.4) | collective-permute-done | bytes 131104 | tf_op jit(solution)/shard_map/ppermute | solution.py:15
  60.7 2.7 %collective-permute-start.6 = (f32[16,1,192]{2,0,1:T(8,128)S(1)}, f32[16,1,192]{2,0,1:T(8,128)S(1)}, u32[]{:S(2)}, u32[]{:S(2)}) collective-permute-start(f32[16,1,192]{2,0,1:T(8,128)S(1)} %get-tuple-element.116), channel_id=1, source_target_pairs={{0,1},{1,2},{2,3},{3,4},{4,5},{5,6},{6,7},{8,9},{9,10},{10,11},{11... | collective-permute-start | bytes 36872 | tf_op jit(solution)/shard_map/ppermute | solution.py:15
  63.5 3.1 %collective-permute-start.7 = (f32[16,1,192]{2,0,1:T(8,128)S(1)}, f32[16,1,192]{2,0,1:T(8,128)S(1)}, u32[]{:S(2)}, u32[]{:S(2)}) collective-permute-start(f32[16,1,192]{2,0,1:T(8,128)S(1)} %get-tuple-element.117), channel_id=1, source_target_pairs={{1,0},{2,1},{3,2},{4,3},{5,4},{6,5},{7,6},{9,8},{10,9},{11,10},{12... | collective-permute-start | bytes 36872 | tf_op jit(solution)/shard_map/ppermute | solution.py:18
  66.6 4.6 %collective-permute-done.7 = f32[16,1,192]{2,0,1:T(8,128)S(1)} collective-permute-done((f32[16,1,192]{2,0,1:T(8,128)S(1)}, f32[16,1,192]{2,0,1:T(8,128)S(1)}, u32[]{:S(2)}, u32[]{:S(2)}) %collective-permute-start.7) | collective-permute-done | bytes 12320 | tf_op jit(solution)/shard_map/ppermute | solution.py:18
  72.1 4.5 %multiply_add_fusion = f32[16,64,128]{2,0,1:T(8,128)S(1)} fusion(f32[16,64,128]{2,0,1:T(8,128)S(1)} %get-tuple-element.187, f32[16,65,192]{2,0,1:T(8,128)S(1)} %get-tuple-element.115, f32[16,65,192]{2,0,1:T(8,128)S(1)} %get-tuple-element.114, f32[16]{0:T(128)S(1)} %get-tuple-element.158, f32[16]{0:T(128)S(1)} %get-tuple-element.159, ...), kind=kLoop, calls=%fused_computation.248 | loop fusion | flops 7995392 | bytes 10749632 | tf_op jit(solution)/shard_map/add | solution.py:33
  78.5 3.0 %multiply_reduce_fusion.18 = (f32[16]{0:T(128)S(1)}, f32[16]{0:T(128)S(1)}, f32[16]{0:T(128)S(1)}, f32[16]{0:T(128)S(1)}, f32[16]{0:T(128)S(1)}, /*index=5*/f32[...) fusion(f32[16,65,192]{2,0,1:T(8,128)S(1)} %get-tuple-element.11, ...), kind=kOutput, calls=%fused_computation.210 | convolution fusion | flops 29884128 | bytes 10487936 | tf_op jit(solution)/shard_map/oc,owt->cwt/dot_general | solution.py:105
  82.7 4.1 %collective-permute-start.8 = (f32[16,64,32]{2,0,1:T(8,128)}, f32[16,64,32]{2,0,1:T(8,128)}, u32[]{:S(2)}, u32[]{:S(2)}) collective-permute-start(f32[16,64,32]{2,0,1:T(8,128)} %get-tuple-element.124), channel_id=1, source_target_pairs={{0,8},{8,16},{16,24},{24,32},{32,40},{40,48},{48,56},{56,64},{64,7... | collective-permute-start | bytes 393224 | tf_op jit(solution)/shard_map/ppermute | solution.py:15
  86.8 4.7 %collective-permute-start.9 = (f32[16,64,32]{2,0,1:T(8,128)}, f32[16,64,32]{2,0,1:T(8,128)}, u32[]{:S(2)}, u32[]{:S(2)}) collective-permute-start(f32[16,64,32]{2,0,1:T(8,128)} %get-tuple-element.125), channel_id=1, source_target_pairs={{8,0},{16,8},{24,16},{32,24},{40,32},{48,40},{56,48},{64,56},{72,6... | collective-permute-start | bytes 393224 | tf_op jit(solution)/shard_map/ppermute | solution.py:18
  91.5 4.9 %multiply_reduce_fusion.9 = (f32[16]{0:T(128)S(1)}, f32[16]{0:T(128)S(1)}, f32[16]{0:T(128)S(1)}, f32[16]{0:T(128)S(1)}, f32[16]{0:T(128)S(1)}, /*index=5*/f32[1...) fusion(f32[16,64,128]{2,0,1:T(8,128)} %copy-done.3, f32[16,64,32]{2,0,1:T(8,128)} %copy-done.8, ...), kind=kLoop, calls=%fused_computation.201 | loop fusion | flops 3932016 | bytes 1835584 | tf_op jit(solution)/shard_map/reduce_sum | solution.py:52
  96.5 2.0 convolution_bitcast_fusion.2
  100.4 4.2 %collective-permute-start.10 = (f32[16,1,192]{2,0,1:T(8,128)S(1)}, f32[16,1,192]{2,0,1:T(8,128)S(1)}, u32[]{:S(2)}, u32[]{:S(2)}) collective-permute-start(f32[16,1,192]{2,0,1:T(8,128)S(1)} %get-tuple-element.112), channel_id=1, source_target_pairs={{0,1},{1,2},{2,3},{3,4},{4,5},{5,6},{6,7},{8,9},{9,10},{10,11},{11... | collective-permute-start | bytes 36872 | tf_op jit(solution)/shard_map/ppermute | solution.py:15
  107.5 4.8 %collective-permute-done.11 = f32[16,1,192]{2,0,1:T(8,128)S(1)} collective-permute-done((f32[16,1,192]{2,0,1:T(8,128)S(1)}, f32[16,1,192]{2,0,1:T(8,128)S(1)}, u32[]{:S(2)}, u32[]{:S(2)}) %collective-permute-start.11) | collective-permute-done | bytes 12320 | tf_op jit(solution)/shard_map/ppermute | solution.py:18
  112.3 2.4 maximum_maximum_fusion.2
  114.8 6.4 %fusion.99 = (f32[16]{0:T(128)S(1)}, f32[16,64,128]{2,0,1:T(8,128)S(1)}) fusion(f32[16,64,128]{2,0,1:T(8,128)S(1)} %copy-done.12, f32[16,65,192]{2,0,1:T(8,128)S(1)} %get-tuple-element.111, f32[16]{0:T(128)S(1)} %get-tuple-element.133, f32[16]{0:T(128)S(1)} %get-tuple-element.152, f32[16]{0:T(128)S(1)} %get-tuple-element.157, f32[16]{0:T(128)S(1)} %get-tuple-element.156, ...), kind=kLoop, calls=%fused_computation.333 | loop fusion | flops 9175024 | bytes 11273984 | tf_op jit(solution)/shard_map/reduce_sum | solution.py:112
  122.0 3.0 %multiply_reduce_fusion.45 = (f32[16]{0:T(128)S(1)}, f32[16]{0:T(128)S(1)}, f32[16]{0:T(128)S(1)}, f32[16]{0:T(128)S(1)}, f32[16]{0:T(128)S(1)}, /*index=5*/f32[...) fusion(f32[16,65,192]{2,0,1:T(8,128)S(1)} %get-tuple-element.11, ...), kind=kOutput, calls=%fused_computation.237 | convolution fusion | flops 29884128 | bytes 10487936 | tf_op jit(solution)/shard_map/oc,owt->cwt/dot_general | solution.py:113
  126.2 3.7 %collective-permute-start.12 = (f32[16,64,32]{2,0,1:T(8,128)}, f32[16,64,32]{2,0,1:T(8,128)S(1)}, u32[]{:S(2)}, u32[]{:S(2)}) collective-permute-start(f32[16,64,32]{2,0,1:T(8,128)} %get-tuple-element.122), channel_id=1, source_target_pairs={{0,8},{8,16},{16,24},{24,32},{32,40},{40,48},{48,56},{56,64},{64,7... | collective-permute-start | bytes 393224 | tf_op jit(solution)/shard_map/ppermute | solution.py:15
  129.9 4.8 %collective-permute-start.13 = (f32[16,64,32]{2,0,1:T(8,128)}, f32[16,64,32]{2,0,1:T(8,128)}, u32[]{:S(2)}, u32[]{:S(2)}) collective-permute-start(f32[16,64,32]{2,0,1:T(8,128)} %get-tuple-element.123), channel_id=1, source_target_pairs={{8,0},{16,8},{24,16},{32,24},{40,32},{48,40},{56,48},{64,56},{72,6... | collective-permute-start | bytes 393224 | tf_op jit(solution)/shard_map/ppermute | solution.py:18
  134.8 2.9 %multiply_reduce_fusion.36 = (f32[16]{0:T(128)S(1)}, f32[16]{0:T(128)S(1)}, f32[16]{0:T(128)S(1)}, f32[16]{0:T(128)S(1)}, f32[16]{0:T(128)S(1)}, /*index=5*/f32[...) fusion(f32[16,64,128]{2,0,1:T(8,128)S(1)} %get-tuple-element.189, f32[16,64,160]{2,0,1:T(8,128)S(1)} %copy-done.2, ...), kind=kLoop, calls=%fused_computation.228 | loop fusion | flops 2883440 | bytes 3801664 | tf_op jit(solution)/shard_map/reduce_sum | solution.py:52
  137.8 98.3 %all-reduce = (f32[16,3,9]{0,2,1:T(8,128)S(1)}, f32[16,16]{1,0:T(8,128)S(1)}, f32[16]{0:T(128)S(1)}, f32[16,3,9]{0,2,1:T(8,128)S(1)}, f32[16,16]{1,0:T(8,128)S(1)}, /*index=5*/f32[16]{0:T(128)S(1)}) all-reduce(f32[16,3,9]{0,2,1:T(8,128)S(1)} %pad_maximum_fusion.11, ...), channel_id=1, replica_groups=mesh['tick'=64,'wire'=8] {'tick','wire'}, use_global_device_ids=true, to_apply=%region_27.28 | all-reduce | flops 1408 | bytes 11264 | tf_op jit(solution)/shard_map/psum | solution.py:120
  237.5 5.0 %collective-permute-start.14 = (f32[16,1,192]{2,0,1:T(8,128)S(1)}, f32[16,1,192]{2,0,1:T(8,128)S(1)}, u32[]{:S(2)}, u32[]{:S(2)}) collective-permute-start(f32[16,1,192]{2,0,1:T(8,128)S(1)} %get-tuple-element.108), channel_id=1, source_target_pairs={{0,1},{1,2},{2,3},{3,4},{4,5},{5,6},{6,7},{8,9},{9,10},{10,11},{11... | collective-permute-start | bytes 36872 | tf_op jit(solution)/shard_map/ppermute | solution.py:15
  242.4 2.1 collective-permute-start.15
  246.3 3.8 %collective-permute-done.15 = f32[16,1,192]{2,0,1:T(8,128)S(1)} collective-permute-done((f32[16,1,192]{2,0,1:T(8,128)S(1)}, f32[16,1,192]{2,0,1:T(8,128)S(1)}, u32[]{:S(2)}, u32[]{:S(2)}) %collective-permute-start.15) | collective-permute-done | bytes 12320 | tf_op jit(solution)/shard_map/ppermute | solution.py:18
  250.2 2.1 maximum_maximum_fusion.3
  252.3 5.7 %fusion.14 = f32[16,64,128]{2,0,1:T(8,128)S(1)} fusion(f32[16,64,128]{2,0,1:T(8,128)S(1)} %get-tuple-element.189, f32[16,64,32]{2,0,1:T(8,128)} %collective-permute-done.13, f32[16,64,32]{2,0,1:T(8,128)S(1)} %collective-permute-done.12, f32[16,65,192]{2,0,1:T(8,128)S(1)} %get-tuple-element.107, f32[16,65,192]{2,0,1:T(8,128)S(1)} %get-tuple-element.106, ...), kind=kLoop, calls=%fused_computation.70 | loop fusion | flops 7995392 | bytes 10749632 | tf_op jit(solution)/shard_map/add | solution.py:33
  (88 shorter events, 24.0 us)
Async XLA Ops:
  0.6 76.0 %copy-start = (f32[16,16]{1,0:T(8,128)S(1)}, f32[16,16]{1,0:T(8,128)}, u32[]{:S(2)}) copy-start(f32[16,16]{1,0:T(8,128)} %param.13) | copy-start | bytes 3076
  2.0 12.4 %copy-start.15 = (f32[16,3,9]{0,1,2:T(4,128)S(1)}, f32[16,3,9]{0,1,2:T(4,128)}, u32[]{:S(2)}) copy-start(f32[16,3,9]{0,1,2:T(4,128)} %param.9) | copy-start | bytes 5188
  2.2 21.8 %collective-permute-start = (f32[16,64,32]{2,0,1:T(8,128)S(1)}, f32[16,64,32]{2,0,1:T(8,128)S(1)}, u32[]{:S(2)}, u32[]{:S(2)}) collective-permute-start(f32[16,64,32]{2,0,1:T(8,128)S(1)} %get-tuple-element.131), channel_id=1, source_target_pairs={{0,8},{8,16},{16,24},{24,32},{32,40},{40,48},{48,56},{56,64},{64,7... | collective-permute-start | bytes 393224 | tf_op jit(solution)/shard_map/ppermute | solution.py:15
  4.1 21.2 %collective-permute-start.1 = (f32[16,64,32]{2,0,1:T(8,128)S(1)}, f32[16,64,32]{2,0,1:T(8,128)S(1)}, u32[]{:S(2)}, u32[]{:S(2)}) collective-permute-start(f32[16,64,32]{2,0,1:T(8,128)S(1)} %get-tuple-element.132), channel_id=1, source_target_pairs={{8,0},{16,8},{24,16},{32,24},{40,32},{48,40},{56,48},{64,56},{72,6... | collective-permute-start | bytes 393224 | tf_op jit(solution)/shard_map/ppermute | solution.py:18
  24.0 12.9 %copy-start.5 = (f32[16,64,32]{2,0,1:T(8,128)}, f32[16,64,32]{2,0,1:T(8,128)S(1)}, u32[]{:S(2)}) copy-start(f32[16,64,32]{2,0,1:T(8,128)S(1)} %collective-permute-done) | copy-start | bytes 393220
  25.4 5.9 %collective-permute-start.2 = (f32[16,1,192]{2,0,1:T(8,128)S(1)}, f32[16,1,192]{2,0,1:T(8,128)S(1)}, u32[]{:S(2)}, u32[]{:S(2)}) collective-permute-start(f32[16,1,192]{2,0,1:T(8,128)S(1)} %get-tuple-element.120), channel_id=1, source_target_pairs={{0,1},{1,2},{2,3},{3,4},{4,5},{5,6},{6,7},{8,9},{9,10},{10,11},{11... | collective-permute-start | bytes 36872 | tf_op jit(solution)/shard_map/ppermute | solution.py:15
  28.3 7.7 %collective-permute-start.3 = (f32[16,1,192]{2,0,1:T(8,128)S(1)}, f32[16,1,192]{2,0,1:T(8,128)S(1)}, u32[]{:S(2)}, u32[]{:S(2)}) collective-permute-start(f32[16,1,192]{2,0,1:T(8,128)S(1)} %get-tuple-element.121), channel_id=1, source_target_pairs={{1,0},{2,1},{3,2},{4,3},{5,4},{6,5},{7,6},{9,8},{10,9},{11,10},{12... | collective-permute-start | bytes 36872 | tf_op jit(solution)/shard_map/ppermute | solution.py:18
  31.3 5.7 %copy-start.1 = (f32[16,64,160]{2,0,1:T(8,128)}, f32[16,64,160]{2,0,1:T(8,128)S(1)}, u32[]{:S(2)}) copy-start(f32[16,64,160]{2,0,1:T(8,128)S(1)} %constant_dynamic-update-slice_fusion) | copy-start | bytes 1966084
  37.0 4.0 %copy-start.18 = (f32[16,16]{1,0:T(8,128)S(1)}, f32[16,16]{1,0:T(8,128)}, u32[]{:S(2)}) copy-start(f32[16,16]{1,0:T(8,128)} %param.10) | copy-start | bytes 3076
  42.4 8.8 %copy-start.16 = (f32[16,3,9]{0,1,2:T(4,128)S(1)}, f32[16,3,9]{0,1,2:T(4,128)}, u32[]{:S(2)}) copy-start(f32[16,3,9]{0,1,2:T(4,128)} %param.12) | copy-start | bytes 5188
  42.6 16.5 %collective-permute-start.4 = (f32[16,64,32]{2,0,1:T(8,128)S(1)}, f32[16,64,32]{2,0,1:T(8,128)S(1)}, u32[]{:S(2)}, u32[]{:S(2)}) collective-permute-start(f32[16,64,32]{2,0,1:T(8,128)S(1)} %get-tuple-element.127), channel_id=1, source_target_pairs={{0,8},{8,16},{16,24},{24,32},{32,40},{40,48},{48,56},{56,64},{64,7... | collective-permute-start | bytes 393224 | tf_op jit(solution)/shard_map/ppermute | solution.py:15
  45.1 15.6 %collective-permute-start.5 = (f32[16,64,32]{2,0,1:T(8,128)S(1)}, f32[16,64,32]{2,0,1:T(8,128)S(1)}, u32[]{:S(2)}, u32[]{:S(2)}) collective-permute-start(f32[16,64,32]{2,0,1:T(8,128)S(1)} %get-tuple-element.128), channel_id=1, source_target_pairs={{8,0},{16,8},{24,16},{32,24},{40,32},{48,40},{56,48},{64,56},{72,6... | collective-permute-start | bytes 393224 | tf_op jit(solution)/shard_map/ppermute | solution.py:18
  59.1 13.0 %copy-start.7 = (f32[16,64,32]{2,0,1:T(8,128)}, f32[16,64,32]{2,0,1:T(8,128)S(1)}, u32[]{:S(2)}) copy-start(f32[16,64,32]{2,0,1:T(8,128)S(1)} %collective-permute-done.4) | copy-start | bytes 393220
  60.7 11.4 %copy-start.8 = (f32[16,64,32]{2,0,1:T(8,128)}, f32[16,64,32]{2,0,1:T(8,128)S(1)}, u32[]{:S(2)}) copy-start(f32[16,64,32]{2,0,1:T(8,128)S(1)} %collective-permute-done.5) | copy-start | bytes 393220
  60.7 5.9 %collective-permute-start.6 = (f32[16,1,192]{2,0,1:T(8,128)S(1)}, f32[16,1,192]{2,0,1:T(8,128)S(1)}, u32[]{:S(2)}, u32[]{:S(2)}) collective-permute-start(f32[16,1,192]{2,0,1:T(8,128)S(1)} %get-tuple-element.116), channel_id=1, source_target_pairs={{0,1},{1,2},{2,3},{3,4},{4,5},{5,6},{6,7},{8,9},{9,10},{10,11},{11... | collective-permute-start | bytes 36872 | tf_op jit(solution)/shard_map/ppermute | solution.py:15
  63.5 7.7 %collective-permute-start.7 = (f32[16,1,192]{2,0,1:T(8,128)S(1)}, f32[16,1,192]{2,0,1:T(8,128)S(1)}, u32[]{:S(2)}, u32[]{:S(2)}) collective-permute-start(f32[16,1,192]{2,0,1:T(8,128)S(1)} %get-tuple-element.117), channel_id=1, source_target_pairs={{1,0},{2,1},{3,2},{4,3},{5,4},{6,5},{7,6},{9,8},{10,9},{11,10},{12... | collective-permute-start | bytes 36872 | tf_op jit(solution)/shard_map/ppermute | solution.py:18
  72.1 4.5 %copy-start.17 = (f32[16,64,128]{2,1,0:T(8,128)S(1)}, f32[16,64,128]{2,1,0:T(8,128)}, u32[]{:S(2)}) copy-start(f32[16,64,128]{2,1,0:T(8,128)} %param.15) | copy-start | bytes 1572868
  72.1 4.5 %copy-start.20 = (f32[16]{0:T(128)S(1)}, f32[16]{0:T(128)}, u32[]{:S(2)}) copy-start(f32[16]{0:T(128)} %param.14) | copy-start | bytes 196
  81.5 9.9 %copy-start.3 = (f32[16,64,128]{2,0,1:T(8,128)}, f32[16,64,128]{2,0,1:T(8,128)S(1)}, u32[]{:S(2)}) copy-start(f32[16,64,128]{2,0,1:T(8,128)S(1)} %get-tuple-element.190) | copy-start | bytes 1572868
  82.7 15.8 %collective-permute-start.8 = (f32[16,64,32]{2,0,1:T(8,128)}, f32[16,64,32]{2,0,1:T(8,128)}, u32[]{:S(2)}, u32[]{:S(2)}) collective-permute-start(f32[16,64,32]{2,0,1:T(8,128)} %get-tuple-element.124), channel_id=1, source_target_pairs={{0,8},{8,16},{16,24},{24,32},{32,40},{40,48},{48,56},{56,64},{64,7... | collective-permute-start | bytes 393224 | tf_op jit(solution)/shard_map/ppermute | solution.py:15
  86.8 12.8 %collective-permute-start.9 = (f32[16,64,32]{2,0,1:T(8,128)}, f32[16,64,32]{2,0,1:T(8,128)}, u32[]{:S(2)}, u32[]{:S(2)}) collective-permute-start(f32[16,64,32]{2,0,1:T(8,128)} %get-tuple-element.125), channel_id=1, source_target_pairs={{8,0},{16,8},{24,16},{32,24},{40,32},{48,40},{56,48},{64,56},{72,6... | collective-permute-start | bytes 393224 | tf_op jit(solution)/shard_map/ppermute | solution.py:18
  98.5 8.0 %copy-start.13 = (f32[16,64,128]{2,0,1:T(8,128)S(1)}, f32[16,64,128]{2,0,1:T(8,128)}, u32[]{:S(2)}) copy-start(f32[16,64,128]{2,0,1:T(8,128)} %get-tuple-element.126) | copy-start | bytes 1572868
  100.4 7.1 %collective-permute-start.10 = (f32[16,1,192]{2,0,1:T(8,128)S(1)}, f32[16,1,192]{2,0,1:T(8,128)S(1)}, u32[]{:S(2)}, u32[]{:S(2)}) collective-permute-start(f32[16,1,192]{2,0,1:T(8,128)S(1)} %get-tuple-element.112), channel_id=1, source_target_pairs={{0,1},{1,2},{2,3},{3,4},{4,5},{5,6},{6,7},{8,9},{9,10},{10,11},{11... | collective-permute-start | bytes 36872 | tf_op jit(solution)/shard_map/ppermute | solution.py:15
  104.6 7.7 %collective-permute-start.11 = (f32[16,1,192]{2,0,1:T(8,128)S(1)}, f32[16,1,192]{2,0,1:T(8,128)S(1)}, u32[]{:S(2)}, u32[]{:S(2)}) collective-permute-start(f32[16,1,192]{2,0,1:T(8,128)S(1)} %get-tuple-element.113), channel_id=1, source_target_pairs={{1,0},{2,1},{3,2},{4,3},{5,4},{6,5},{7,6},{9,8},{10,9},{11,10},{12... | collective-permute-start | bytes 36872 | tf_op jit(solution)/shard_map/ppermute | solution.py:18
  107.5 7.3 %copy-start.12 = (f32[16,64,128]{2,0,1:T(8,128)S(1)}, f32[16,64,128]{2,0,1:T(8,128)}, u32[]{:S(2)}) copy-start(f32[16,64,128]{2,0,1:T(8,128)} %get-tuple-element.188) | copy-start | bytes 1572868
  114.8 6.4 %copy-start.10 = (f32[16,64,128]{2,0,1:T(8,128)S(1)}, f32[16,64,128]{2,0,1:T(8,128)}, u32[]{:S(2)}) copy-start(f32[16,64,128]{2,0,1:T(8,128)} %copy-done.9) | copy-start | bytes 1572868
  125.0 9.7 %copy-start.2 = (f32[16,64,160]{2,0,1:T(8,128)S(1)}, f32[16,64,160]{2,0,1:T(8,128)}, u32[]{:S(2)}) copy-start(f32[16,64,160]{2,0,1:T(8,128)} %copy-done.1) | copy-start | bytes 1966084
  125.0 9.7 %copy-start.6 = (f32[16,64,32]{2,0,1:T(8,128)S(1)}, f32[16,64,32]{2,0,1:T(8,128)}, u32[]{:S(2)}) copy-start(f32[16,64,32]{2,0,1:T(8,128)} %copy-done.5) | copy-start | bytes 393220
  126.2 110.5 %collective-permute-start.12 = (f32[16,64,32]{2,0,1:T(8,128)}, f32[16,64,32]{2,0,1:T(8,128)S(1)}, u32[]{:S(2)}, u32[]{:S(2)}) collective-permute-start(f32[16,64,32]{2,0,1:T(8,128)} %get-tuple-element.122), channel_id=1, source_target_pairs={{0,8},{8,16},{16,24},{24,32},{32,40},{40,48},{48,56},{56,64},{64,7... | collective-permute-start | bytes 393224 | tf_op jit(solution)/shard_map/ppermute | solution.py:15
  129.9 106.8 %collective-permute-start.13 = (f32[16,64,32]{2,0,1:T(8,128)}, f32[16,64,32]{2,0,1:T(8,128)}, u32[]{:S(2)}, u32[]{:S(2)}) collective-permute-start(f32[16,64,32]{2,0,1:T(8,128)} %get-tuple-element.123), channel_id=1, source_target_pairs={{8,0},{16,8},{24,16},{32,24},{40,32},{48,40},{56,48},{64,56},{72,6... | collective-permute-start | bytes 393224 | tf_op jit(solution)/shard_map/ppermute | solution.py:18
  237.5 8.9 %collective-permute-start.14 = (f32[16,1,192]{2,0,1:T(8,128)S(1)}, f32[16,1,192]{2,0,1:T(8,128)S(1)}, u32[]{:S(2)}, u32[]{:S(2)}) collective-permute-start(f32[16,1,192]{2,0,1:T(8,128)S(1)} %get-tuple-element.108), channel_id=1, source_target_pairs={{0,1},{1,2},{2,3},{3,4},{4,5},{5,6},{6,7},{8,9},{9,10},{10,11},{11... | collective-permute-start | bytes 36872 | tf_op jit(solution)/shard_map/ppermute | solution.py:15
  242.4 7.7 %collective-permute-start.15 = (f32[16,1,192]{2,0,1:T(8,128)S(1)}, f32[16,1,192]{2,0,1:T(8,128)S(1)}, u32[]{:S(2)}, u32[]{:S(2)}) collective-permute-start(f32[16,1,192]{2,0,1:T(8,128)S(1)} %get-tuple-element.109), channel_id=1, source_target_pairs={{1,0},{2,1},{3,2},{4,3},{5,4},{6,5},{7,6},{9,8},{10,9},{11,10},{12... | collective-permute-start | bytes 36872 | tf_op jit(solution)/shard_map/ppermute | solution.py:18
  (5 other events, 13.4 us)
where the time goes:
time: 260 us; the launch traced here: 259 us
  blocking collectives  98.3 us (38%)
  starting transfers between devices  62.9 us (24%)
  waiting for transfers between devices  39.3 us (15%)
  other arithmetic  37.6 us (14%)
  matrix products  12.1 us (5%)
  local copies, waits for them, and re-layouts  7.58 us (3%)
    psum x1, blocking collectives, per_device(): lax.psum((gkern_front, gmix_front, gbias_front, gkern_back, gmix_back, gb...  98.3 us
    ppermute x8, starting transfers between devices, with_halo(): lax.ppermute(lax.slice_in_dim(block, 0, width, axis=dim), axis, backward)  36 us
    ppermute x8, starting transfers between devices, with_halo(): lax.ppermute(lax.slice_in_dim(block, block.shape[dim] - width, None, axis...  26.9 us
    ppermute x8, waiting for transfers between devices, with_halo(): lax.ppermute(lax.slice_in_dim(block, 0, width, axis=dim), axis, backward)  21.9 us
    ppermute x8, waiting for transfers between devices, with_halo(): lax.ppermute(lax.slice_in_dim(block, block.shape[dim] - width, None, axis...  17.5 us
    add x3, other arithmetic, depthwise(): total_sum + kernel_weight[:, row_index, column_index][:, None, None] * pa...  14.2 us
    reduce_sum x2, other arithmetic, tap_grads(): jnp.sum(upward_gradient * padded_input[:, row_index:row_index + row_count...  7.79 us
    reduce_sum x1, other arithmetic, per_device(): gbias_front = jnp.sum(grad_front, axis=(1, 2))  6.43 us
  transfers between devices with their start and end apart: 16, of which 9 were waited for; matrix products, arithmetic and copies ran while one was open for 5% of the time, Pallas kernels for 0%

commit v1 on v0

--- a/solution.py
+++ b/solution.py
@@ -118,7 +118,8 @@
         spread(under_front, kernel_extent, 1), kernel_front[:, ::-1, ::-1], row_count, column_count
     )
     totals = lax.psum(
-        (gkern_front, gmix_front, gbias_front, gkern_back, gmix_back, gbias_back), ("tick", "wire")
+        lax.psum((gkern_front, gmix_front, gbias_front, gkern_back, gmix_back, gbias_back), "wire"),
+        "tick",
     )
     factor = 1.0 / math.sqrt(
         row_count * lax.axis_size("wire") * column_count * lax.axis_size("tick")

time: 260 us -> 474 us (1.82)
  the two profiles are of different devices: /device:TPU:30 before, /device:TPU:38 now
where the time goes in v1:
time: 474 us; the launch traced here: 473 us
  blocking collectives  308 us (65%)
  starting transfers between devices  67.6 us (14%)
  waiting for transfers between devices  38.7 us (8%)
  other arithmetic  37.6 us (8%)
  matrix products  12.1 us (3%)
  local copies, waits for them, and re-layouts  7.58 us (2%)
    psum x1, blocking collectives, per_device(): lax.psum(lax.psum((gkern_front, gmix_front, gbias_front, gkern_back, gmix...  275 us
    ppermute x8, starting transfers between devices, with_halo(): lax.ppermute(lax.slice_in_dim(block, 0, width, axis=dim), axis, backward)  44.2 us
    psum x1, blocking collectives, per_device(): lax.psum((gkern_front, gmix_front, gbias_front, gkern_back, gmix_back, gb...  33.3 us
    ppermute x8, starting transfers between devices, with_halo(): lax.ppermute(lax.slice_in_dim(block, block.shape[dim] - width, None, axis...  23.4 us
    ppermute x8, waiting for transfers between devices, with_halo(): lax.ppermute(lax.slice_in_dim(block, 0, width, axis=dim), axis, backward)  20.9 us
    ppermute x8, waiting for transfers between devices, with_halo(): lax.ppermute(lax.slice_in_dim(block, block.shape[dim] - width, None, axis...  17.7 us
    add x3, other arithmetic, depthwise(): total_sum + kernel_weight[:, row_index, column_index][:, None, None] * pa...  14.2 us
  transfers between devices with their start and end apart: 16, of which 8 were waited for; matrix products, arithmetic and copies ran while one was open for 3% of the time, Pallas kernels for 0%

profile of v1, /device:TPU:38, one launch (start us, length us, event | category | flops | bytes accessed | tf_op | source)
XLA Modules:
  0.0 473.1 jit_solution(9498058100045949811)
XLA Ops:
  4.1 10.3 %collective-permute-start.1 = (f32[16,64,32]{2,0,1:T(8,128)S(1)}, f32[16,64,32]{2,0,1:T(8,128)S(1)}, u32[]{:S(2)}, u32[]{:S(2)}) collective-permute-start(f32[16,64,32]{2,0,1:T(8,128)S(1)} %get-tuple-element.138), channel_id=1, source_target_pairs={{8,0},{16,8},{24,16},{32,24},{40,32},{48,40},{56,48},{64,56},{72,6... | collective-permute-start | bytes 393224 | tf_op jit(solution)/shard_map/ppermute | solution.py:18
  14.5 10.5 %collective-permute-done = f32[16,64,32]{2,0,1:T(8,128)S(1)} collective-permute-done((f32[16,64,32]{2,0,1:T(8,128)S(1)}, f32[16,64,32]{2,0,1:T(8,128)S(1)}, u32[]{:S(2)}, u32[]{:S(2)}) %collective-permute-start) | collective-permute-done | bytes 131104 | tf_op jit(solution)/shard_map/ppermute | solution.py:15
  25.0 3.0 collective-permute-start.2
  28.0 2.9 collective-permute-start.3
  31.0 4.8 %collective-permute-done.3 = f32[16,1,192]{2,0,1:T(8,128)S(1)} collective-permute-done((f32[16,1,192]{2,0,1:T(8,128)S(1)}, f32[16,1,192]{2,0,1:T(8,128)S(1)}, u32[]{:S(2)}, u32[]{:S(2)}) %collective-permute-start.3) | collective-permute-done | bytes 12320 | tf_op jit(solution)/shard_map/ppermute | solution.py:18
  36.7 3.9 multiply_add_fusion.1
  42.3 2.7 collective-permute-start.4
  45.0 7.1 %collective-permute-start.5 = (f32[16,64,32]{2,0,1:T(8,128)S(1)}, f32[16,64,32]{2,0,1:T(8,128)S(1)}, u32[]{:S(2)}, u32[]{:S(2)}) collective-permute-start(f32[16,64,32]{2,0,1:T(8,128)S(1)} %get-tuple-element.134), channel_id=1, source_target_pairs={{8,0},{16,8},{24,16},{32,24},{40,32},{48,40},{56,48},{64,56},{72,6... | collective-permute-start | bytes 393224 | tf_op jit(solution)/shard_map/ppermute | solution.py:18
  52.1 7.2 %collective-permute-done.4 = f32[16,64,32]{2,0,1:T(8,128)S(1)} collective-permute-done((f32[16,64,32]{2,0,1:T(8,128)S(1)}, f32[16,64,32]{2,0,1:T(8,128)S(1)}, u32[]{:S(2)}, u32[]{:S(2)}) %collective-permute-start.4) | collective-permute-done | bytes 131104 | tf_op jit(solution)/shard_map/ppermute | solution.py:15
  59.4 2.3 collective-permute-done.5
  61.7 2.5 collective-permute-start.6
  64.3 3.3 collective-permute-start.7
  67.6 4.4 collective-permute-done.7
  72.9 4.5 multiply_add_fusion
  79.3 3.0 multiply_reduce_fusion.18
  83.5 2.7 collective-permute-start.8
  86.1 7.3 %collective-permute-start.9 = (f32[16,64,32]{2,0,1:T(8,128)}, f32[16,64,32]{2,0,1:T(8,128)}, u32[]{:S(2)}, u32[]{:S(2)}) collective-permute-start(f32[16,64,32]{2,0,1:T(8,128)} %get-tuple-element.131), channel_id=1, source_target_pairs={{8,0},{16,8},{24,16},{32,24},{40,32},{48,40},{56,48},{64,56},{72,6... | collective-permute-start | bytes 393224 | tf_op jit(solution)/shard_map/ppermute | solution.py:18
  93.5 4.9 %multiply_reduce_fusion.9 = (f32[16]{0:T(128)S(1)}, f32[16]{0:T(128)S(1)}, f32[16]{0:T(128)S(1)}, f32[16]{0:T(128)S(1)}, f32[16]{0:T(128)S(1)}, /*index=5*/f32[1...) fusion(f32[16,64,128]{2,0,1:T(8,128)} %copy-done.3, f32[16,64,32]{2,0,1:T(8,128)} %copy-done.8, ...), kind=kLoop, calls=%fused_computation.201 | loop fusion | flops 3932016 | bytes 1835584 | tf_op jit(solution)/shard_map/reduce_sum | solution.py:52
  100.5 2.3 collective-permute-done.9
  103.6 2.4 collective-permute-start.10
  106.1 3.4 collective-permute-start.11
  110.5 3.4 collective-permute-done.11
  113.8 2.4 maximum_maximum_fusion.2
  116.3 6.4 %fusion.99 = (f32[16]{0:T(128)S(1)}, f32[16,64,128]{2,0,1:T(8,128)S(1)}) fusion(f32[16,64,128]{2,0,1:T(8,128)S(1)} %copy-done.12, f32[16,65,192]{2,0,1:T(8,128)S(1)} %get-tuple-element.117, f32[16]{0:T(128)S(1)} %get-tuple-element.139, f32[16]{0:T(128)S(1)} %get-tuple-element.158, f32[16]{0:T(128)S(1)} %get-tuple-element.163, f32[16]{0:T(128)S(1)} %get-tuple-element.162, ...), kind=kLoop, calls=%fused_computation.333 | loop fusion | flops 9175024 | bytes 11273984 | tf_op jit(solution)/shard_map/reduce_sum | solution.py:112
  123.5 3.0 multiply_reduce_fusion.45
  129.6 7.9 %collective-permute-start.13 = (f32[16,64,32]{2,0,1:T(8,128)}, f32[16,64,32]{2,0,1:T(8,128)}, u32[]{:S(2)}, u32[]{:S(2)}) collective-permute-start(f32[16,64,32]{2,0,1:T(8,128)} %get-tuple-element.129), channel_id=1, source_target_pairs={{8,0},{16,8},{24,16},{32,24},{40,32},{48,40},{56,48},{64,56},{72,6... | collective-permute-start | bytes 393224 | tf_op jit(solution)/shard_map/ppermute | solution.py:18
  137.5 2.9 multiply_reduce_fusion.36
  140.5 33.3 %all-reduce.1 = (f32[16,3,9]{0,2,1:T(8,128)S(1)}, f32[16,16]{1,0:T(8,128)S(1)}, f32[16]{0:T(128)S(1)}, f32[16,3,9]{0,2,1:T(8,128)S(1)}, f32[16,16]{1,0:T(8,128)S(1)}, /*index=5*/f32[16]{0:T(128)S(1)}) all-reduce(f32[16,3,9]{0,2,1:T(8,128)S(1)} %pad_maximum_fusion.11, ...), channel_id=1, replica_groups=mesh['tick'=64,'wire'=8] {'wire'}, use_global_device_ids=true, to_apply=%region_27.28 | all-reduce | flops 1408 | bytes 11264 | tf_op jit(solution)/shard_map/psum | solution.py:121
  173.8 275.0 %all-reduce = (f32[16,3,9]{0,2,1:T(8,128)S(1)}, f32[16,16]{1,0:T(8,128)S(1)}, f32[16]{0:T(128)S(1)}, f32[16,3,9]{0,2,1:T(8,128)S(1)}, f32[16,16]{1,0:T(8,128)S(1)}, /*index=5*/f32[16]{0:T(128)S(1)}) all-reduce(f32[16,3,9]{0,2,1:T(8,128)S(1)} %get-tuple-element.102, ...), channel_id=1, replica_groups=mesh['tick'=64,'wire'=8] {'tick'}, use_global_device_ids=true, to_apply=%region_28.29 | all-reduce | flops 1408 | bytes 11264 | tf_op jit(solution)/shard_map/psum | solution.py:120
  450.3 6.3 %collective-permute-start.14 = (f32[16,1,192]{2,0,1:T(8,128)S(1)}, f32[16,1,192]{2,0,1:T(8,128)S(1)}, u32[]{:S(2)}, u32[]{:S(2)}) collective-permute-start(f32[16,1,192]{2,0,1:T(8,128)S(1)} %get-tuple-element.114), channel_id=1, source_target_pairs={{0,1},{1,2},{2,3},{3,4},{4,5},{5,6},{6,7},{8,9},{9,10},{10,11},{11... | collective-permute-start | bytes 36872 | tf_op jit(solution)/shard_map/ppermute | solution.py:15
  460.5 3.8 collective-permute-done.15
  466.4 5.7 %fusion.14 = f32[16,64,128]{2,0,1:T(8,128)S(1)} fusion(f32[16,64,128]{2,0,1:T(8,128)S(1)} %get-tuple-element.195, f32[16,64,32]{2,0,1:T(8,128)} %collective-permute-done.13, f32[16,64,32]{2,0,1:T(8,128)S(1)} %collective-permute-done.12, f32[16,65,192]{2,0,1:T(8,128)S(1)} %get-tuple-element.113, f32[16,65,192]{2,0,1:T(8,128)S(1)} %get-tuple-element.112, ...), kind=kLoop, calls=%fused_computation.70 | loop fusion | flops 7995392 | bytes 10749632 | tf_op jit(solution)/shard_map/add | solution.py:33
  (89 shorter events, 26.3 us)
Async XLA Ops:
  0.6 76.8 %copy-start = (f32[16,16]{1,0:T(8,128)S(1)}, f32[16,16]{1,0:T(8,128)}, u32[]{:S(2)}) copy-start(f32[16,16]{1,0:T(8,128)} %param.13) | copy-start | bytes 3076
  2.0 12.4 %copy-start.15 = (f32[16,3,9]{0,1,2:T(4,128)S(1)}, f32[16,3,9]{0,1,2:T(4,128)}, u32[]{:S(2)}) copy-start(f32[16,3,9]{0,1,2:T(4,128)} %param.9) | copy-start | bytes 5188
  2.2 22.7 %collective-permute-start = (f32[16,64,32]{2,0,1:T(8,128)S(1)}, f32[16,64,32]{2,0,1:T(8,128)S(1)}, u32[]{:S(2)}, u32[]{:S(2)}) collective-permute-start(f32[16,64,32]{2,0,1:T(8,128)S(1)} %get-tuple-element.137), channel_id=1, source_target_pairs={{0,8},{8,16},{16,24},{24,32},{32,40},{40,48},{48,56},{56,64},{64,7... | collective-permute-start | bytes 393224 | tf_op jit(solution)/shard_map/ppermute | solution.py:15
  4.1 20.8 %collective-permute-start.1 = (f32[16,64,32]{2,0,1:T(8,128)S(1)}, f32[16,64,32]{2,0,1:T(8,128)S(1)}, u32[]{:S(2)}, u32[]{:S(2)}) collective-permute-start(f32[16,64,32]{2,0,1:T(8,128)S(1)} %get-tuple-element.138), channel_id=1, source_target_pairs={{8,0},{16,8},{24,16},{32,24},{40,32},{48,40},{56,48},{64,56},{72,6... | collective-permute-start | bytes 393224 | tf_op jit(solution)/shard_map/ppermute | solution.py:18
  25.0 11.7 %copy-start.5 = (f32[16,64,32]{2,0,1:T(8,128)}, f32[16,64,32]{2,0,1:T(8,128)S(1)}, u32[]{:S(2)}) copy-start(f32[16,64,32]{2,0,1:T(8,128)S(1)} %collective-permute-done) | copy-start | bytes 393220
  25.0 5.9 %collective-permute-start.2 = (f32[16,1,192]{2,0,1:T(8,128)S(1)}, f32[16,1,192]{2,0,1:T(8,128)S(1)}, u32[]{:S(2)}, u32[]{:S(2)}) collective-permute-start(f32[16,1,192]{2,0,1:T(8,128)S(1)} %get-tuple-element.126), channel_id=1, source_target_pairs={{0,1},{1,2},{2,3},{3,4},{4,5},{5,6},{6,7},{8,9},{9,10},{10,11},{11... | collective-permute-start | bytes 36872 | tf_op jit(solution)/shard_map/ppermute | solution.py:15
  28.0 7.7 %collective-permute-start.3 = (f32[16,1,192]{2,0,1:T(8,128)S(1)}, f32[16,1,192]{2,0,1:T(8,128)S(1)}, u32[]{:S(2)}, u32[]{:S(2)}) collective-permute-start(f32[16,1,192]{2,0,1:T(8,128)S(1)} %get-tuple-element.127), channel_id=1, source_target_pairs={{1,0},{2,1},{3,2},{4,3},{5,4},{6,5},{7,6},{9,8},{10,9},{11,10},{12... | collective-permute-start | bytes 36872 | tf_op jit(solution)/shard_map/ppermute | solution.py:18
  31.0 5.7 %copy-start.1 = (f32[16,64,160]{2,0,1:T(8,128)}, f32[16,64,160]{2,0,1:T(8,128)S(1)}, u32[]{:S(2)}) copy-start(f32[16,64,160]{2,0,1:T(8,128)S(1)} %constant_dynamic-update-slice_fusion) | copy-start | bytes 1966084
  42.1 10.0 %copy-start.16 = (f32[16,3,9]{0,1,2:T(4,128)S(1)}, f32[16,3,9]{0,1,2:T(4,128)}, u32[]{:S(2)}) copy-start(f32[16,3,9]{0,1,2:T(4,128)} %param.12) | copy-start | bytes 5188
  42.3 17.1 %collective-permute-start.4 = (f32[16,64,32]{2,0,1:T(8,128)S(1)}, f32[16,64,32]{2,0,1:T(8,128)S(1)}, u32[]{:S(2)}, u32[]{:S(2)}) collective-permute-start(f32[16,64,32]{2,0,1:T(8,128)S(1)} %get-tuple-element.133), channel_id=1, source_target_pairs={{0,8},{8,16},{16,24},{24,32},{32,40},{40,48},{48,56},{56,64},{64,7... | collective-permute-start | bytes 393224 | tf_op jit(solution)/shard_map/ppermute | solution.py:15
  45.0 16.7 %collective-permute-start.5 = (f32[16,64,32]{2,0,1:T(8,128)S(1)}, f32[16,64,32]{2,0,1:T(8,128)S(1)}, u32[]{:S(2)}, u32[]{:S(2)}) collective-permute-start(f32[16,64,32]{2,0,1:T(8,128)S(1)} %get-tuple-element.134), channel_id=1, source_target_pairs={{8,0},{16,8},{24,16},{32,24},{40,32},{48,40},{56,48},{64,56},{72,6... | collective-permute-start | bytes 393224 | tf_op jit(solution)/shard_map/ppermute | solution.py:18
  59.4 13.5 %copy-start.7 = (f32[16,64,32]{2,0,1:T(8,128)}, f32[16,64,32]{2,0,1:T(8,128)S(1)}, u32[]{:S(2)}) copy-start(f32[16,64,32]{2,0,1:T(8,128)S(1)} %collective-permute-done.4) | copy-start | bytes 393220
  61.6 11.3 %copy-start.8 = (f32[16,64,32]{2,0,1:T(8,128)}, f32[16,64,32]{2,0,1:T(8,128)S(1)}, u32[]{:S(2)}) copy-start(f32[16,64,32]{2,0,1:T(8,128)S(1)} %collective-permute-done.5) | copy-start | bytes 393220
  61.7 5.9 %collective-permute-start.6 = (f32[16,1,192]{2,0,1:T(8,128)S(1)}, f32[16,1,192]{2,0,1:T(8,128)S(1)}, u32[]{:S(2)}, u32[]{:S(2)}) collective-permute-start(f32[16,1,192]{2,0,1:T(8,128)S(1)} %get-tuple-element.122), channel_id=1, source_target_pairs={{0,1},{1,2},{2,3},{3,4},{4,5},{5,6},{6,7},{8,9},{9,10},{10,11},{11... | collective-permute-start | bytes 36872 | tf_op jit(solution)/shard_map/ppermute | solution.py:15
  64.3 7.7 %collective-permute-start.7 = (f32[16,1,192]{2,0,1:T(8,128)S(1)}, f32[16,1,192]{2,0,1:T(8,128)S(1)}, u32[]{:S(2)}, u32[]{:S(2)}) collective-permute-start(f32[16,1,192]{2,0,1:T(8,128)S(1)} %get-tuple-element.123), channel_id=1, source_target_pairs={{1,0},{2,1},{3,2},{4,3},{5,4},{6,5},{7,6},{9,8},{10,9},{11,10},{12... | collective-permute-start | bytes 36872 | tf_op jit(solution)/shard_map/ppermute | solution.py:18
  72.9 4.5 copy-start.17
  72.9 4.5 copy-start.20
  82.3 11.1 %copy-start.3 = (f32[16,64,128]{2,0,1:T(8,128)}, f32[16,64,128]{2,0,1:T(8,128)S(1)}, u32[]{:S(2)}) copy-start(f32[16,64,128]{2,0,1:T(8,128)S(1)} %get-tuple-element.196) | copy-start | bytes 1572868
  83.5 17.0 %collective-permute-start.8 = (f32[16,64,32]{2,0,1:T(8,128)}, f32[16,64,32]{2,0,1:T(8,128)}, u32[]{:S(2)}, u32[]{:S(2)}) collective-permute-start(f32[16,64,32]{2,0,1:T(8,128)} %get-tuple-element.130), channel_id=1, source_target_pairs={{0,8},{8,16},{16,24},{24,32},{32,40},{40,48},{48,56},{56,64},{64,7... | collective-permute-start | bytes 393224 | tf_op jit(solution)/shard_map/ppermute | solution.py:15
  86.1 16.6 %collective-permute-start.9 = (f32[16,64,32]{2,0,1:T(8,128)}, f32[16,64,32]{2,0,1:T(8,128)}, u32[]{:S(2)}, u32[]{:S(2)}) collective-permute-start(f32[16,64,32]{2,0,1:T(8,128)} %get-tuple-element.131), channel_id=1, source_target_pairs={{8,0},{16,8},{24,16},{32,24},{40,32},{48,40},{56,48},{64,56},{72,6... | collective-permute-start | bytes 393224 | tf_op jit(solution)/shard_map/ppermute | solution.py:18
  98.4 4.4 copy-start.4
  100.5 9.0 %copy-start.13 = (f32[16,64,128]{2,0,1:T(8,128)S(1)}, f32[16,64,128]{2,0,1:T(8,128)}, u32[]{:S(2)}) copy-start(f32[16,64,128]{2,0,1:T(8,128)} %get-tuple-element.132) | copy-start | bytes 1572868
  103.6 6.8 %collective-permute-start.10 = (f32[16,1,192]{2,0,1:T(8,128)S(1)}, f32[16,1,192]{2,0,1:T(8,128)S(1)}, u32[]{:S(2)}, u32[]{:S(2)}) collective-permute-start(f32[16,1,192]{2,0,1:T(8,128)S(1)} %get-tuple-element.118), channel_id=1, source_target_pairs={{0,1},{1,2},{2,3},{3,4},{4,5},{5,6},{6,7},{8,9},{9,10},{10,11},{11... | collective-permute-start | bytes 36872 | tf_op jit(solution)/shard_map/ppermute | solution.py:15
  106.1 7.7 %collective-permute-start.11 = (f32[16,1,192]{2,0,1:T(8,128)S(1)}, f32[16,1,192]{2,0,1:T(8,128)S(1)}, u32[]{:S(2)}, u32[]{:S(2)}) collective-permute-start(f32[16,1,192]{2,0,1:T(8,128)S(1)} %get-tuple-element.119), channel_id=1, source_target_pairs={{1,0},{2,1},{3,2},{4,3},{5,4},{6,5},{7,6},{9,8},{10,9},{11,10},{12... | collective-permute-start | bytes 36872 | tf_op jit(solution)/shard_map/ppermute | solution.py:18
  110.5 5.8 %copy-start.12 = (f32[16,64,128]{2,0,1:T(8,128)S(1)}, f32[16,64,128]{2,0,1:T(8,128)}, u32[]{:S(2)}) copy-start(f32[16,64,128]{2,0,1:T(8,128)} %get-tuple-element.194) | copy-start | bytes 1572868
  116.3 6.4 %copy-start.10 = (f32[16,64,128]{2,0,1:T(8,128)S(1)}, f32[16,64,128]{2,0,1:T(8,128)}, u32[]{:S(2)}) copy-start(f32[16,64,128]{2,0,1:T(8,128)} %copy-done.9) | copy-start | bytes 1572868
  126.5 11.0 %copy-start.2 = (f32[16,64,160]{2,0,1:T(8,128)S(1)}, f32[16,64,160]{2,0,1:T(8,128)}, u32[]{:S(2)}) copy-start(f32[16,64,160]{2,0,1:T(8,128)} %copy-done.1) | copy-start | bytes 1966084
  126.5 11.0 %copy-start.6 = (f32[16,64,32]{2,0,1:T(8,128)S(1)}, f32[16,64,32]{2,0,1:T(8,128)}, u32[]{:S(2)}) copy-start(f32[16,64,32]{2,0,1:T(8,128)} %copy-done.5) | copy-start | bytes 393220
  127.7 321.8 %collective-permute-start.12 = (f32[16,64,32]{2,0,1:T(8,128)}, f32[16,64,32]{2,0,1:T(8,128)S(1)}, u32[]{:S(2)}, u32[]{:S(2)}) collective-permute-start(f32[16,64,32]{2,0,1:T(8,128)} %get-tuple-element.128), channel_id=1, source_target_pairs={{0,8},{8,16},{16,24},{24,32},{32,40},{40,48},{48,56},{56,64},{64,7... | collective-permute-start | bytes 393224 | tf_op jit(solution)/shard_map/ppermute | solution.py:15
  129.6 319.9 %collective-permute-start.13 = (f32[16,64,32]{2,0,1:T(8,128)}, f32[16,64,32]{2,0,1:T(8,128)}, u32[]{:S(2)}, u32[]{:S(2)}) collective-permute-start(f32[16,64,32]{2,0,1:T(8,128)} %get-tuple-element.129), channel_id=1, source_target_pairs={{8,0},{16,8},{24,16},{32,24},{40,32},{48,40},{56,48},{64,56},{72,6... | collective-permute-start | bytes 393224 | tf_op jit(solution)/shard_map/ppermute | solution.py:18
  450.3 10.2 %collective-permute-start.14 = (f32[16,1,192]{2,0,1:T(8,128)S(1)}, f32[16,1,192]{2,0,1:T(8,128)S(1)}, u32[]{:S(2)}, u32[]{:S(2)}) collective-permute-start(f32[16,1,192]{2,0,1:T(8,128)S(1)} %get-tuple-element.114), channel_id=1, source_target_pairs={{0,1},{1,2},{2,3},{3,4},{4,5},{5,6},{6,7},{8,9},{9,10},{10,11},{11... | collective-permute-start | bytes 36872 | tf_op jit(solution)/shard_map/ppermute | solution.py:15
  456.6 7.7 %collective-permute-start.15 = (f32[16,1,192]{2,0,1:T(8,128)S(1)}, f32[16,1,192]{2,0,1:T(8,128)S(1)}, u32[]{:S(2)}, u32[]{:S(2)}) collective-permute-start(f32[16,1,192]{2,0,1:T(8,128)S(1)} %get-tuple-element.115), channel_id=1, source_target_pairs={{1,0},{2,1},{3,2},{4,3},{5,4},{6,5},{7,6},{9,8},{10,9},{11,10},{12... | collective-permute-start | bytes 36872 | tf_op jit(solution)/shard_map/ppermute | solution.py:18
  (5 other events, 14.2 us)
